TPU v7x, 32 devices: a whole 2x2x4 slice. The times are simulated.
32 devices in a mesh: groups: 1, seq: 16 (over z, y, x), section: 1, head: 2 (over core).
Axes of the slice: x: 2, y: 2, z: 4, core: 2. Of those that a mesh axis runs over, the one named last changes fastest.
Arguments:
- queries: bfloat16 [2560, 3072], P(('groups', 'seq', 'head'), 'section'), may hold values from -24 to 24
- keys: bfloat16 [2560, 3072], P(('groups', 'seq', 'head'), 'section'), may hold values from -10.5 to 10.5
- values: bfloat16 [2560, 3072], P(('groups', 'seq', 'head'), 'section'), may hold values from -6 to 6
- text_keys: bfloat16 [128, 3072], P(('groups', 'seq', 'head'), 'section'), may hold values from -10 to 10
- text_values: bfloat16 [128, 3072], P(('groups', 'seq', 'head'), 'section'), may hold values from -6 to 6
- text_length: int32 [1], P('groups'), may hold values from 32 to 128
- out_weight: bfloat16 [3072, 3072], P(None, 'section'), may hold values from -0.109375 to 0.109375
Outputs:
- projected: bfloat16 [2560, 3072], P(('groups', 'seq', 'head'), 'section')
All inputs are finite; a program needn't handle non-finite values.
Results may differ from a plain program's by a relative error of at most 0.0065.
Values may be sent and summed in bfloat16 or wider, within the bound.
A program may use at most 128 MiB of HBM per device.

v0:
```python
import functools
import math

import jax
import jax.numpy as jnp
import numpy as np
from jax import lax
from jax.experimental import pallas as pl
from jax.experimental.pallas import tpu as pltpu
from jax.sharding import PartitionSpec as P

HEAD_DIM = 128
MESH = pl.DeviceIdType.MESH


def kernel(
    dims,
    length_ref,
    q_ref,
    k_ref,
    v_ref,
    tk_ref,
    tv_ref,
    order_ref,
    pick_hbm,
    w_hbm,
    o_out,
    qb,
    kv,
    tb,
    tkv,
    ob,
    att,
    wb,
    acc,
    pick_ref,
    o_ref,
    wide,
    packed,
    t_ref,
    local_sem,
    w_sem,
    q_send,
    kv_send,
    t_send,
    o_send,
    q_recv,
    kv_recv,
    t_recv,
    o_recv,
    kv2_send,
    kv2_recv,
    t2_send,
    t2_recv,
):
    A, R, C, X, hp = dims
    d = HEAD_DIM
    rows = q_ref.shape[0]
    seq = lax.axis_index("seq")
    core = lax.axis_index("head")
    section = lax.axis_index("section")
    a = seq // R
    r = lax.rem(seq, R)
    slot = r * C + core
    width = hp * d

    def at(a2=None, r2=None, c2=None, x2=None):
        return {
            "seq": (a if a2 is None else a2) * R + (r if r2 is None else r2),
            "head": core if c2 is None else c2,
            "section": section if x2 is None else x2,
        }

    def cols(start, size):
        return pl.ds(pl.multiple_of(start, d), size)

    def own_rows(which):
        return pl.ds(pl.multiple_of(which * rows, 16), rows)

    barrier = pltpu.get_barrier_semaphore()

    def greet(target):
        pl.semaphore_signal(barrier, inc=1, device_id=target, device_id_type=MESH)

    for da in range(A):
        for dx in range(X):
            if da or dx:
                greet(at(a2=lax.rem(a + da, A), x2=lax.rem(section + dx, X)))
    for dr in range(1, R):
        greet(at(r2=lax.rem(r + dr, R)))
    for dc in range(1, C):
        greet(at(c2=lax.rem(core + dc, C)))
    pl.semaphore_wait(barrier, A * X - 1 + R - 1 + C - 1)

    def remote(src, dst, send, recv, target):
        return pltpu.make_async_remote_copy(
            src_ref=src, dst_ref=dst, send_sem=send, recv_sem=recv, device_id=target, device_id_type=MESH
        )

    def first(j, ref, landing, send, recv):
        src_cols = lambda a2: cols((a2 * hp + j) * d, d)
        pltpu.make_async_copy(ref.at[:, src_cols(a)], landing.at[own_rows(a)], recv).start()

        def one(da, _):
            a2 = lax.rem(a + da, A)
            remote(ref.at[:, src_cols(a2)], landing.at[own_rows(a)], send, recv, at(a2=a2)).start()
            return 0

        lax.fori_loop(1, A, one, 0)

    def first_kv(j, n):
        first(j, (k_ref, v_ref)[n], kv.at[j, n, slot], kv_send.at[j, n], kv_recv.at[j, n])

    def first_q(j):
        first(j, q_ref, qb.at[j], q_send.at[j], q_recv.at[j])

    def first_text():
        count = tk_ref.shape[0]
        if 2 * count < wide.shape[0]:
            wide[...] = jnp.zeros_like(wide)
        wide[:count] = tk_ref[...].astype(jnp.float32)
        wide[count : 2 * count] = tv_ref[...].astype(jnp.float32)
        packed[...] = wide[...].astype(jnp.bfloat16)
        pltpu.sync_copy(packed, t_ref)
        pltpu.make_async_copy(t_ref.at[:, cols(a * width, width)], tb.at[slot, a], t_recv).start()

        def one(da, _):
            a2 = lax.rem(a + da, A)
            remote(t_ref.at[:, cols(a2 * width, width)], tb.at[slot, a], t_send, t_recv, at(a2=a2)).start()
            return 0

        lax.fori_loop(1, A, one, 0)

    for j in range(hp):
        first_kv(j, 0)
        first_kv(j, 1)
        if j == 0:
            first_text()
    for j in range(hp):
        first_q(j)

    pick_copy = pltpu.make_async_copy(pick_hbm, pick_ref, local_sem)
    pick_copy.start()

    weight_copies = []
    for j in range(hp):
        for b in range(X * A):
            weight_copies.append(
                pltpu.make_async_copy(
                    w_hbm.at[pl.ds((b * hp + j) * d, d)], wb.at[j, pl.ds(b * d, d)], w_sem.at[j]
                )
            )
            weight_copies[-1].start()

    def drain(ref, sem):
        pltpu.make_async_copy(ref, ref, sem).wait()

    def members():
        for dr in range(1, R):
            yield dr - 1, at(r2=lax.rem(r + dr, R))
        for dc in range(1, C):
            yield R - 2 + dc, at(c2=lax.rem(core + dc, C))

    def share(block, send, recv):
        for n, target in members():
            remote(block(slot), block(slot), send.at[n], recv.at[n], target).start()

    def forward(block, send, recv):
        base = R - 1 + C - 1
        for dr in range(1, R):
            from_slot = lax.rem(r - dr + R, R) * C + core
            drain(block(from_slot), recv.at[dr - 1])
            for dc in range(1, C):
                n = base + (dr - 1) * (C - 1) + dc - 1
                remote(
                    block(from_slot), block(from_slot), send.at[n], recv.at[n], at(c2=lax.rem(core + dc, C))
                ).start()

    def collect(block, recv):
        base = R - 1 + C - 1
        for dc in range(1, C):
            from_core = lax.rem(core - dc + C, C)
            drain(block(r * C + from_core), recv.at[R - 2 + dc])
            for dr in range(1, R):
                n = base + (dr - 1) * (C - 1) + dc - 1
                drain(block(lax.rem(r - dr + R, R) * C + from_core), recv.at[n])

    def shared_sends(block, send):
        for n in range(R - 1 + C - 1 + (R - 1) * (C - 1)):
            drain(block(slot), send.at[n])

    def kv_block(j, n):
        return lambda s: kv.at[j, n, s]

    def text_block(s):
        return tb.at[s]

    def share_kv(j):
        for n in range(2):
            drain(kv.at[j, n, slot], kv_recv.at[j, n])
            share(kv_block(j, n), kv2_send.at[j, n], kv2_recv.at[j, n])

    def project(j):
        drain(att.at[j], o_recv.at[j])
        drain(wb.at[j], w_sem.at[j])
        columns = o_ref.shape[1]
        step = 768 if columns % 768 == 0 else d

        @pl.loop(0, columns // step)
        def _(i):
            part = pl.ds(pl.multiple_of(i * step, d), step)
            term = jnp.dot(att[j], wb[j, :, part], preferred_element_type=jnp.float32)
            if j > 0:
                term = acc[:, part] + term
            if j < hp - 1:
                acc[:, part] = term
            else:
                o_ref[:, part] = term.astype(o_ref.dtype)

    group = 2 if A % 2 == 0 else 1
    tile = group * rows
    scale = math.log2(math.e) * d ** (-0.5)
    nt = (((1,), (1,)), ((), ()))

    def attend(j, i):
        part = pl.ds(pl.multiple_of(i * tile, 16), tile)
        q = qb[j, part]
        keys = kv[j, 0].reshape(-1, d)
        values = kv[j, 1].reshape(-1, d)
        s1 = lax.dot_general(q, keys, nt, preferred_element_type=jnp.float32)
        s2 = lax.dot_general(q, tkv[j, 0], nt, preferred_element_type=jnp.float32)
        s2 = jnp.where(order_ref[...] < length_ref[0], s2, -1e30)
        top = jnp.maximum(jnp.max(s1, axis=1, keepdims=True), jnp.max(s2, axis=1, keepdims=True))
        p1 = jnp.exp2((s1 - top) * scale)
        p2 = jnp.exp2((s2 - top) * scale)
        total = jnp.sum(p1, axis=1, keepdims=True) + jnp.sum(p2, axis=1, keepdims=True)
        o = jnp.dot(p1.astype(jnp.bfloat16), values, preferred_element_type=jnp.float32)
        o = o + jnp.dot(p2.astype(jnp.bfloat16), tkv[j, 1], preferred_element_type=jnp.float32)
        ob[j, part] = (o / total).astype(jnp.bfloat16)

    column = cols((section * A + a) * d, d)

    def back(j, a2, dx):
        remote(
            ob.at[j, own_rows(a2)],
            att.at[j, :, column],
            o_send.at[j],
            o_recv.at[j],
            at(a2=a2, x2=lax.rem(section + dx, X)),
        ).start()

    def back_group(j, i):
        for b in range(group):
            for dx in range(X):
                back(j, i * group + b, dx)

    def back_own(j, i):
        for b in range(group):
            for dx in range(1, X):
                back(j, i * group + b, dx)
            if group > 1:
                @pl.when(i * group + b != a)
                def _():
                    back(j, i * group + b, 0)
        pltpu.make_async_copy(ob.at[j, own_rows(a)], att.at[j, :, column], o_recv.at[j]).start()

    own = a // group
    groups = A // group

    def attention(j):
        @pl.loop(1, groups)
        def _(di):
            i = lax.rem(own + di, groups)
            attend(j, i)
            back_group(j, i)

        attend(j, own)
        back_own(j, own)

    def forward_kv(j):
        for n in range(2):
            forward(kv_block(j, n), kv2_send.at[j, n], kv2_recv.at[j, n])

    share_kv(0)
    drain(tb.at[slot], t_recv)
    share(text_block, t2_send, t2_recv)
    for j in range(1, hp):
        share_kv(j)
        forward_kv(j - 1)
        if j == 1:
            forward(text_block, t2_send, t2_recv)
    if hp == 1:
        forward(text_block, t2_send, t2_recv)
    collect(text_block, t2_recv)
    pick_copy.wait()
    block = tb[...].reshape(-1, width)
    for n in range(2):
        got = jnp.dot(pick_ref[n], block, preferred_element_type=jnp.float32).astype(jnp.bfloat16)
        for i in range(hp):
            tkv[i, n] = got[:, i * d : (i + 1) * d]
    for j in range(hp):
        if j == hp - 1:
            forward_kv(j)
        drain(qb.at[j], q_recv.at[j])
        for n in range(2):
            collect(kv_block(j, n), kv2_recv.at[j, n])
        attention(j)
    for j in range(hp):
        project(j)
    out_copy = pltpu.make_async_copy(o_ref, o_out, local_sem)
    out_copy.start()

    for j in range(hp):
        for n in range(2):
            if A > 1:
                drain(kv.at[j, n, slot, pl.ds(0, (A - 1) * rows)], kv_send.at[j, n])
            shared_sends(kv_block(j, n), kv2_send.at[j, n])
        if A > 1:
            drain(qb.at[j, pl.ds(0, (A - 1) * rows)], q_send.at[j])
        if A * X > 1:
            drain(att.at[j, :, pl.ds(0, (A * X - 1) * d)], o_send.at[j])
    if A > 1:
        drain(tb.at[slot, pl.ds(0, A - 1)], t_send)
    shared_sends(text_block, t2_send)
    out_copy.wait()


def shards(sizes, queries, keys, values, text_keys, text_values, text_length, out_weight):
    S, C, X = sizes
    rows, columns = queries.shape
    heads = columns // HEAD_DIM
    A = math.gcd(heads, S)
    R = S // A
    hp = heads // A
    text_rows = text_keys.shape[0]
    text = text_rows * S * C
    bf16 = jnp.bfloat16
    pad = -(-2 * text_rows // 8) * 8
    t = np.arange(text)
    block, i = t // text_rows, t % text_rows
    from_slot, from_a = block // A, block % A
    from_r, from_c = from_slot // C, from_slot % C
    order = (((from_a * R + from_r) * C + from_c) * text_rows + i).astype(np.int32)[None, :]
    pick = np.zeros((2, text, R * C * A * pad), np.float32)
    for n in range(2):
        pick[n, t, block * pad + n * text_rows + i] = 1.0
    pick = jnp.asarray(pick, bf16)
    out_columns = out_weight.shape[1]
    shares = R - 1 + C - 1 + (R - 1) * (C - 1)
    vmem = pl.BlockSpec(memory_space=pltpu.VMEM)
    hbm = pl.BlockSpec(memory_space=pl.ANY)
    dma = pltpu.SemaphoreType.DMA
    return pl.pallas_call(
        functools.partial(kernel, (A, R, C, X, hp)),
        out_shape=jax.ShapeDtypeStruct((rows, out_columns), bf16),
        in_specs=[pl.BlockSpec(memory_space=pltpu.SMEM)] + [hbm] * 3 + [vmem] * 3 + [hbm] * 2,
        out_specs=pl.BlockSpec(memory_space=pl.ANY),
        scratch_shapes=[
            pltpu.VMEM((hp, A * rows, HEAD_DIM), bf16),
            pltpu.VMEM((hp, 2, R * C, A * rows, HEAD_DIM), bf16),
            pltpu.VMEM((R * C, A, pad, hp * HEAD_DIM), bf16),
            pltpu.VMEM((hp, 2, text, HEAD_DIM), bf16),
            pltpu.VMEM((hp, A * rows, HEAD_DIM), bf16),
            pltpu.VMEM((hp, rows, X * A * HEAD_DIM), bf16),
            pltpu.VMEM((hp, X * A * HEAD_DIM, out_columns), bf16),
            pltpu.VMEM((rows, out_columns), jnp.float32),
            pltpu.VMEM(pick.shape, bf16),
            pltpu.VMEM((rows, out_columns), bf16),
            pltpu.VMEM((pad, columns), jnp.float32),
            pltpu.VMEM((pad, columns), bf16),
            pltpu.VMEM((pad, columns), bf16),
            dma,
            dma((hp,)),
            dma((hp,)),
            dma((hp, 2)),
            dma,
            dma((hp,)),
            dma((hp,)),
            dma((hp, 2)),
            dma,
            dma((hp,)),
            dma((hp, 2, shares)),
            dma((hp, 2, shares)),
            dma((shares,)),
            dma((shares,)),
        ],
        compiler_params=pltpu.CompilerParams(
            collective_id=0, has_side_effects=True, vmem_limit_bytes=60 * 1024 * 1024
        ),
    )(text_length, queries, keys, values, text_keys, text_values, jnp.asarray(order), pick, out_weight)


def solution(mesh):
    sizes = (mesh.shape["seq"], mesh.shape["head"], mesh.shape["section"])
    tokens = P(("groups", "seq", "head"), "section")
    return jax.shard_map(
        functools.partial(shards, sizes),
        mesh=mesh,
        in_specs=(tokens,) * 5 + (P("groups"), P(None, "section")),
        out_specs=tokens,
        check_vma=False,
    )
```

profile of v0, /device:TPU:1, one launch (start us, length us, event | category | flops | bytes accessed | tf_op | source)
XLA Modules:
  0.0 59.1 jit_solution(8117533461643635574)
XLA Ops:
  0.7 56.6 %shard_map.91 = bf16[80,3072]{1,0:T(8,128)(2,1)} custom-call(s32[1]{0:T(128)S(6)} %copy.11.length_ref, bf16[80,3072]{1,0:T(8,128)(2,1)} %q_ref.1, bf16[80,3072]{1,0:T(8,128)(2,1)} %k_ref.1, bf16[80,3072]{1,0:T(8,128)(2,1)} %v_ref.1, bf16[4,3072]{1,0:T(4,128)(2,1)} %tk_ref.1, bf16[4,3072]{1,0:T(4,128)(2,1)} %tv_ref.1, s32[1,128]{1,0:T(1,128)} %constant.5.clone.order_ref, ...), custom_call_target="tpu_custom_call" | custom-call | tf_op jit(solution)/shard_map/pallas_call | solution.py:353
  57.3 1.8 %copy.12 = bf16[80,3072]{1,0:T(8,128)(2,1)} copy(bf16[80,3072]{1,0:T(8,128)(2,1)} %shard_map.91) | data formatting | bytes 983040
where the time goes:
time: 59.4 us; the launch traced here: 59.1 us
  Pallas kernels  56.6 us (95%)
  local copies, waits for them, and re-layouts  1.84 us (3%)
  between operations  0.66 us (1%)
    pallas_call x1, Pallas kernels, shards(): pl.pallas_call(functools.partial(kernel, (A, R, C, X, hp)), out_shape=jax...  56.6 us
    unnamed x1, local copies, waits for them, and re-layouts  1.84 us

commit v1 on v0

v1 whole, which is shorter than its diff:
```python
import functools
import math

import jax
import jax.numpy as jnp
import numpy as np
from jax import lax
from jax.experimental import pallas as pl
from jax.experimental.pallas import tpu as pltpu
from jax.sharding import PartitionSpec as P

HEAD_DIM = 128
MESH = pl.DeviceIdType.MESH


def kernel(
    dims,
    length_ref,
    q_ref,
    k_ref,
    v_ref,
    tk_ref,
    tv_ref,
    order_ref,
    pick_hbm,
    w_hbm,
    o_ref,
    qb,
    kv,
    tb,
    tkv,
    ob,
    att,
    wb,
    acc,
    pick_ref,
    scores,
    wide,
    packed,
    t_ref,
    local_sem,
    w_sem,
    x_send,
    x_recv,
    t_send,
    t_recv,
    o_send,
    o_recv,
    kv2_send,
    kv2_recv,
    t2_send,
    t2_recv,
    entry,
):
    A, R, C, X, hp, Y, H, group = dims
    d = HEAD_DIM
    rows = q_ref.shape[0]
    Z, HB, G = A // Y, A // H, A // group
    seq = lax.axis_index("seq")
    core = lax.axis_index("head")
    section = lax.axis_index("section")
    a = seq // R
    r = lax.rem(seq, R)
    z, y = a // Y, lax.rem(a, Y)
    slot = r * C + core
    width = hp * d
    own_half = a // HB
    halves = [lax.rem(own_half + h, H) for h in range(H)]

    def at(a2=None, r2=None, c2=None, x2=None):
        return {
            "seq": (a if a2 is None else a2) * R + (r if r2 is None else r2),
            "head": core if c2 is None else c2,
            "section": section if x2 is None else x2,
        }

    def cols(start, size):
        return pl.ds(pl.multiple_of(start, d), size)

    def own_rows(which):
        return pl.ds(pl.multiple_of(which * rows, 16), rows)

    def half_rows(h):
        return pl.ds(pl.multiple_of(h * HB * rows, 16), HB * rows)

    def at_hops(k):
        for dy in range(min(Y - 1, k) + 1):
            dz = k - dy
            y2 = lax.rem(y + dy, Y)
            if dz == 0:
                yield None, z * Y + y2
            elif dz < Z:
                yield z + dz < Z, (z + dz) * Y + y2
                yield z - dz >= 0, (z - dz) * Y + y2

    def each(k, act):
        for there, a2 in at_hops(k):
            if there is None:
                act(a2)
            else:
                pl.when(there)(functools.partial(act, a2))

    hops = Z - 1 + Y - 1
    beside = (z > 0).astype(jnp.int32) + (z < Z - 1).astype(jnp.int32) + Y - 1
    barrier = pltpu.get_barrier_semaphore()

    def greet(target, sem=barrier):
        pl.semaphore_signal(sem, inc=1, device_id=target, device_id_type=MESH)

    staged = False
    if staged:
        each(1, lambda a2: greet(at(a2=a2)))
    else:
        for da in range(A):
            for dx in range(X):
                if da or dx:
                    greet(at(a2=lax.rem(a + da, A), x2=lax.rem(section + dx, X)))
    for dr in range(1, R):
        greet(at(r2=lax.rem(r + dr, R)))
    for dc in range(1, C):
        greet(at(c2=lax.rem(core + dc, C)))

    def remote(src, dst, send, recv, target):
        return pltpu.make_async_remote_copy(
            src_ref=src, dst_ref=dst, send_sem=send, recv_sem=recv, device_id=target, device_id_type=MESH
        )

    def drain(ref, sem):
        pltpu.make_async_copy(ref, ref, sem).wait()

    def landing(j, n):
        return qb.at[j] if n == 2 else kv.at[j, n, slot]

    def first(j, n, a2):
        src = (k_ref, v_ref, q_ref)[n].at[:, cols((a2 * hp + j) * d, d)]
        remote(src, landing(j, n).at[own_rows(a)], x_send, x_recv.at[j, n, own_half], at(a2=a2)).start()

    def first_own(j, n):
        src = (k_ref, v_ref, q_ref)[n].at[:, cols((a * hp + j) * d, d)]
        pltpu.make_async_copy(src, landing(j, n).at[own_rows(a)], x_recv.at[j, n, own_half]).start()

    def first_text(a2):
        remote(t_ref.at[:, cols(a2 * width, width)], tb.at[slot, a], t_send, t_recv, at(a2=a2)).start()

    count = tk_ref.shape[0]
    if 2 * count < wide.shape[0]:
        wide[...] = jnp.zeros_like(wide)
    wide[:count] = tk_ref[...].astype(jnp.float32)
    wide[count : 2 * count] = tv_ref[...].astype(jnp.float32)
    packed[...] = wide[...].astype(jnp.bfloat16)
    text_copy = pltpu.make_async_copy(packed, t_ref, local_sem)
    text_copy.start()
    for n in range(3):
        first_own(0, n)

    if staged:
        pl.semaphore_wait(barrier, beside + R - 1 + C - 1)
    else:
        pl.semaphore_wait(barrier, A * X - 1 + R - 1 + C - 1)
    for k in range(1, hops + 1):
        if staged and k > 1:
            pl.semaphore_wait(entry.at[k - 2], beside)
        if staged and k < hops:
            each(1, lambda a2: greet(at(a2=a2), entry.at[k - 1]))

    def send_all(j, which):
        for n in which:
            for da in range(1, A):
                first(j, n, lax.rem(a + da, A))
            if j > 0:
                first_own(j, n)

    text_copy.wait()
    pltpu.make_async_copy(t_ref.at[:, cols(a * width, width)], tb.at[slot, a], t_recv).start()
    for da in range(1, A):
        first_text(lax.rem(a + da, A))

    send_all(0, (0, 1))
    for j in range(hp):
        if j + 1 < hp:
            send_all(j + 1, (0, 1))
        send_all(j, (2,))

    pick_copy = pltpu.make_async_copy(pick_hbm, pick_ref, local_sem)
    pick_copy.start()
    for j in range(hp):
        for b in range(X * A):
            pltpu.make_async_copy(
                w_hbm.at[pl.ds((b * hp + j) * d, d)], wb.at[j, pl.ds(b * d, d)], w_sem.at[j]
            ).start()

    def members():
        for dr in range(1, R):
            yield dr - 1, at(r2=lax.rem(r + dr, R))
        for dc in range(1, C):
            yield R - 2 + dc, at(c2=lax.rem(core + dc, C))

    def share(block, send, recv):
        for n, target in members():
            remote(block(slot), block(slot), send, recv.at[n], target).start()

    def forward(block, send, recv):
        base = R - 1 + C - 1
        for dr in range(1, R):
            from_slot = lax.rem(r - dr + R, R) * C + core
            drain(block(from_slot), recv.at[dr - 1])
            for dc in range(1, C):
                n = base + (dr - 1) * (C - 1) + dc - 1
                remote(
                    block(from_slot), block(from_slot), send, recv.at[n], at(c2=lax.rem(core + dc, C))
                ).start()

    def collect(block, recv):
        base = R - 1 + C - 1
        for dc in range(1, C):
            from_core = lax.rem(core - dc + C, C)
            drain(block(r * C + from_core), recv.at[R - 2 + dc])
            for dr in range(1, R):
                n = base + (dr - 1) * (C - 1) + dc - 1
                drain(block(lax.rem(r - dr + R, R) * C + from_core), recv.at[n])

    def kv_block(j, n, h):
        return lambda s: kv.at[j, n, s, half_rows(h)]

    def text_block(s):
        return tb.at[s]

    def kv_sems(j, n, h):
        return kv2_send, kv2_recv.at[j, n, h]

    def share_kv(j, h):
        for n in range(2):
            drain(kv.at[j, n, slot, half_rows(h)], x_recv.at[j, n, h])
            share(kv_block(j, n, h), *kv_sems(j, n, h))

    def forward_kv(j, h):
        for n in range(2):
            forward(kv_block(j, n, h), *kv_sems(j, n, h))

    def collect_kv(j):
        for h in halves:
            for n in range(2):
                collect(kv_block(j, n, h), kv_sems(j, n, h)[1])

    def wait_q(j):
        for h in halves:
            drain(qb.at[j, half_rows(h)], x_recv.at[j, 2, h])

    def project(j, parts):
        for g in parts:
            drain(att.at[j, :, pl.ds(0, X * group * d)], o_recv.at[j, g])
        columns = o_ref.shape[1]
        step = 768 if columns % 768 == 0 else d
        if len(parts) == G:
            pieces = [pl.ds(0, X * A * d)]
        else:
            pieces = [cols((x * A + g * group) * d, group * d) for g in parts for x in range(X)]

        def run(first_term, last_term):
            @pl.loop(0, columns // step)
            def _(i):
                part = pl.ds(pl.multiple_of(i * step, d), step)
                term = None if first_term else acc[:, part]
                for piece in pieces:
                    got = jnp.dot(att[j, :, piece], wb[j, piece, part], preferred_element_type=jnp.float32)
                    term = got if term is None else term + got
                if last_term:
                    o_ref[:, part] = term.astype(o_ref.dtype)
                else:
                    acc[:, part] = term

        return run

    scale = math.log2(math.e) * d ** (-0.5)
    nt = (((1,), (1,)), ((), ()))
    total_keys = R * C * A * rows
    span = next((n for n in (640, 512, 256, 128) if total_keys % n == 0), total_keys)

    def lanes(x, combine, start):
        for c in range(0, x.shape[1], d):
            start = combine(start, x[:, c : c + d])
        return start

    def flat(j, n, s):
        return kv[j, n].reshape(-1, d)[s * span : (s + 1) * span]

    def attend(j):
        q = qb[j]
        text_scores = lax.dot_general(q, tkv[j, 0], nt, preferred_element_type=jnp.float32)
        text_scores = jnp.where(order_ref[...] < length_ref[0], text_scores, -1e30)
        top = lanes(text_scores[:, d:], jnp.maximum, text_scores[:, :d])
        for s in range(total_keys // span):
            part = lax.dot_general(q, flat(j, 0, s), nt, preferred_element_type=jnp.float32)
            scores[:, s * span : (s + 1) * span] = part
            top = lanes(part, jnp.maximum, top)
        top = jnp.max(top, axis=1, keepdims=True)
        p = jnp.exp2((text_scores - top) * scale)
        total = lanes(p[:, d:], jnp.add, p[:, :d])
        o = jnp.dot(p.astype(jnp.bfloat16), tkv[j, 1], preferred_element_type=jnp.float32)
        for s in range(total_keys // span):
            p = jnp.exp2((scores[:, s * span : (s + 1) * span] - top) * scale)
            total = lanes(p, jnp.add, total)
            o = o + jnp.dot(p.astype(jnp.bfloat16), flat(j, 1, s), preferred_element_type=jnp.float32)
        total = jnp.sum(total, axis=1, keepdims=True)
        ob[j] = (o / total).astype(jnp.bfloat16)

    column = cols((section * A + a) * d, d)
    own = a // group

    def back(j, a2, dx):
        remote(
            ob.at[j, own_rows(a2)],
            att.at[j, :, column],
            o_send,
            o_recv.at[j, own],
            at(a2=a2, x2=lax.rem(section + dx, X)),
        ).start()

    def back_group(j, i):
        for b in range(group):
            a2 = i * group + b
            for dx in range(1, X):
                back(j, a2, dx)

            @pl.when(a2 != a)
            def _():
                back(j, a2, 0)

            @pl.when(a2 == a)
            def _():
                pltpu.make_async_copy(ob.at[j, own_rows(a2)], att.at[j, :, column], o_recv.at[j, own]).start()

    def tile_at(k):
        if G & (G - 1):
            return lax.rem(own + 1 + k, G)
        across = jnp.where(own < G // 2, G - 1 - k, k)
        return jnp.where(k < G // 2, across, own ^ (G - 1 - k))

    def part_at(k):
        return lax.rem(own + k, G) if G & (G - 1) else own ^ k

    def attention(j):
        attend(j)

        @pl.loop(0, G)
        def _(k):
            back_group(j, tile_at(k))

    drain(tb.at[slot], t_recv)
    share(text_block, t2_send, t2_recv)
    for h in halves:
        share_kv(0, h)
    forward(text_block, t2_send, t2_recv)
    if hp > 1:
        for h in halves:
            share_kv(1, h)
    for h in halves:
        forward_kv(0, h)
    collect(text_block, t2_recv)
    pick_copy.wait()
    block = tb[...].reshape(-1, width)
    for n in range(2):
        got = jnp.dot(pick_ref[n], block, preferred_element_type=jnp.float32).astype(jnp.bfloat16)
        for i in range(hp):
            tkv[i, n] = got[:, i * d : (i + 1) * d]
    for j in range(hp):
        wait_q(j)
        collect_kv(j)
        attention(j)
        if j + 1 < hp:
            for h in halves:
                forward_kv(j + 1, h)
        if j + 2 < hp:
            for h in halves:
                share_kv(j + 2, h)
    for j in range(hp - 1):
        drain(wb.at[j], w_sem.at[j])
        project(j, list(range(G)))(j == 0, False)
    drain(wb.at[hp - 1], w_sem.at[hp - 1])
    others = R * C - 1
    if others:
        drain(kv.at[:, :, pl.ds(0, others)], kv2_send)
        drain(tb.at[pl.ds(0, others)], t2_send)
    if A > 1:
        for n in range(3):
            drain(qb.at[:, pl.ds(0, (A - 1) * rows)], x_send)
        drain(tb.at[slot, pl.ds(0, A - 1)], t_send)
    if G % 2:
        project(hp - 1, list(range(G)))(hp == 1, True)
    else:
        project(hp - 1, [part_at(k) for k in range(G // 2)])(hp == 1, False)
        project(hp - 1, [part_at(k) for k in range(G // 2, G)])(False, True)
    if A * X > 1:
        drain(att.at[:, :, pl.ds(0, (A * X - 1) * d)], o_send)


def shards(sizes, queries, keys, values, text_keys, text_values, text_length, out_weight):
    S, C, X = sizes
    rows, columns = queries.shape
    heads = columns // HEAD_DIM
    A = math.gcd(heads, S)
    R = S // A
    hp = heads // A
    text_rows = text_keys.shape[0]
    text = text_rows * S * C
    bf16 = jnp.bfloat16
    pad = -(-2 * text_rows // 8) * 8
    t = np.arange(text)
    block, i = t // text_rows, t % text_rows
    from_slot, from_a = block // A, block % A
    from_r, from_c = from_slot // C, from_slot % C
    order = (((from_a * R + from_r) * C + from_c) * text_rows + i).astype(np.int32)[None, :]
    pick = np.zeros((2, text, R * C * A * pad), np.float32)
    for n in range(2):
        pick[n, t, block * pad + n * text_rows + i] = 1.0
    pick = jnp.asarray(pick, bf16)
    out_columns = out_weight.shape[1]
    shares = R - 1 + C - 1 + (R - 1) * (C - 1)
    Y = H = group = 2 if A % 2 == 0 else 1
    vmem = pl.BlockSpec(memory_space=pltpu.VMEM)
    hbm = pl.BlockSpec(memory_space=pl.ANY)
    dma = pltpu.SemaphoreType.DMA
    return pl.pallas_call(
        functools.partial(kernel, (A, R, C, X, hp, Y, H, group)),
        out_shape=pltpu.VMEM((rows, out_columns), bf16),
        in_specs=[pl.BlockSpec(memory_space=pltpu.SMEM)] + [hbm] * 3 + [vmem] * 3 + [hbm] * 2,
        out_specs=vmem,
        scratch_shapes=[
            pltpu.VMEM((hp, A * rows, HEAD_DIM), bf16),
            pltpu.VMEM((hp, 2, R * C, A * rows, HEAD_DIM), bf16),
            pltpu.VMEM((R * C, A, pad, hp * HEAD_DIM), bf16),
            pltpu.VMEM((hp, 2, text, HEAD_DIM), bf16),
            pltpu.VMEM((hp, A * rows, HEAD_DIM), bf16),
            pltpu.VMEM((hp, rows, X * A * HEAD_DIM), bf16),
            pltpu.VMEM((hp, X * A * HEAD_DIM, out_columns), bf16),
            pltpu.VMEM((rows, out_columns), jnp.float32),
            pltpu.VMEM(pick.shape, bf16),
            pltpu.VMEM((A * rows, R * C * A * rows), jnp.float32),
            pltpu.VMEM((pad, columns), jnp.float32),
            pltpu.VMEM((pad, columns), bf16),
            pltpu.VMEM((pad, columns), bf16),
            dma,
            dma((hp,)),
            dma,
            dma((hp, 3, H)),
            dma,
            dma,
            dma,
            dma((hp, A // group)),
            dma,
            dma((hp, 2, H, shares)),
            dma,
            dma((shares,)),
            pltpu.SemaphoreType.REGULAR((A,)),
        ],
        compiler_params=pltpu.CompilerParams(
            collective_id=0, has_side_effects=True, vmem_limit_bytes=60 * 1024 * 1024
        ),
    )(text_length, queries, keys, values, text_keys, text_values, jnp.asarray(order), pick, out_weight)


def solution(mesh):
    sizes = (mesh.shape["seq"], mesh.shape["head"], mesh.shape["section"])
    tokens = P(("groups", "seq", "head"), "section")
    return jax.shard_map(
        functools.partial(shards, sizes),
        mesh=mesh,
        in_specs=(tokens,) * 5 + (P("groups"), P(None, "section")),
        out_specs=tokens,
        check_vma=False,
    )
```

time: 59.4 us -> 56.9 us (0.958)
  Pallas kernels: 56.6 us -> 55.3 us
  local copies, waits for them, and re-layouts: 1.84 us -> 0.78 us
    pallas_call x1, Pallas kernels: 56.6 us -> 55.3 us  [shards(): pl.pallas_call(functools.partial(kernel, (A, R, C, X, hp, Y, H, group)),...]
    unnamed x1, local copies, waits for them, and re-layouts: 1.84 us -> 0.78 us
where the time goes in v1:
time: 56.9 us; the launch traced here: 56.8 us
  Pallas kernels  55.3 us (97%)
  local copies, waits for them, and re-layouts  0.78 us (1%)
  between operations  0.66 us (1%)
    pallas_call x1, Pallas kernels, shards(): pl.pallas_call(functools.partial(kernel, (A, R, C, X, hp, Y, H, group)),...  55.3 us

profile of v1, /device:TPU:1, one launch (start us, length us, event | category | flops | bytes accessed | tf_op | source)
XLA Modules:
  0.0 56.8 jit_solution(9321524280907177405)
XLA Ops:
  0.7 55.3 %shard_map.91 = bf16[80,3072]{1,0:T(8,128)(2,1)S(1)} custom-call(s32[1]{0:T(128)S(6)} %copy.12.length_ref, bf16[80,3072]{1,0:T(8,128)(2,1)} %q_ref.1, bf16[80,3072]{1,0:T(8,128)(2,1)} %k_ref.1, bf16[80,3072]{1,0:T(8,128)(2,1)} %v_ref.1, bf16[4,3072]{1,0:T(4,128)(2,1)} %tk_ref.1, bf16[4,3072]{1,0:T(4,128)(2,1)} %tv_ref.1, s32[1,128]{1,0:T(1,128)} %constant.5.clone.order_ref, ...), custom_call_target="tpu_custom_call" | custom-call | tf_op jit(solution)/shard_map/pallas_call | solution.py:423
  56.0 0.8 %copy.11 = bf16[80,3072]{1,0:T(8,128)(2,1)} copy(bf16[80,3072]{1,0:T(8,128)(2,1)S(1)} %shard_map.91) | data formatting | bytes 983040

commit v2 on v1

--- a/solution.py
+++ b/solution.py
@@ -19,9 +19,9 @@
     q_ref,
     k_ref,
     v_ref,
-    tk_ref,
-    tv_ref,
-    order_ref,
+    tk_hbm,
+    tv_hbm,
+    order_hbm,
     pick_hbm,
     w_hbm,
     o_ref,
@@ -35,10 +35,14 @@
     acc,
     pick_ref,
     scores,
+    tk_ref,
+    tv_ref,
+    order_ref,
     wide,
     packed,
     t_ref,
     local_sem,
+    early_sem,
     w_sem,
     x_send,
     x_recv,
@@ -50,18 +54,16 @@
     kv2_recv,
     t2_send,
     t2_recv,
-    entry,
 ):
-    A, R, C, X, hp, Y, H, group = dims
+    A, R, C, X, hp, H, group = dims
     d = HEAD_DIM
     rows = q_ref.shape[0]
-    Z, HB, G = A // Y, A // H, A // group
+    HB, G = A // H, A // group
     seq = lax.axis_index("seq")
     core = lax.axis_index("head")
     section = lax.axis_index("section")
     a = seq // R
     r = lax.rem(seq, R)
-    z, y = a // Y, lax.rem(a, Y)
     slot = r * C + core
     width = hp * d
     own_half = a // HB
@@ -83,38 +85,15 @@
     def half_rows(h):
         return pl.ds(pl.multiple_of(h * HB * rows, 16), HB * rows)
 
-    def at_hops(k):
-        for dy in range(min(Y - 1, k) + 1):
-            dz = k - dy
-            y2 = lax.rem(y + dy, Y)
-            if dz == 0:
-                yield None, z * Y + y2
-            elif dz < Z:
-                yield z + dz < Z, (z + dz) * Y + y2
-                yield z - dz >= 0, (z - dz) * Y + y2
-
-    def each(k, act):
-        for there, a2 in at_hops(k):
-            if there is None:
-                act(a2)
-            else:
-                pl.when(there)(functools.partial(act, a2))
-
-    hops = Z - 1 + Y - 1
-    beside = (z > 0).astype(jnp.int32) + (z < Z - 1).astype(jnp.int32) + Y - 1
     barrier = pltpu.get_barrier_semaphore()
 
-    def greet(target, sem=barrier):
-        pl.semaphore_signal(sem, inc=1, device_id=target, device_id_type=MESH)
-
-    staged = False
-    if staged:
-        each(1, lambda a2: greet(at(a2=a2)))
-    else:
-        for da in range(A):
-            for dx in range(X):
-                if da or dx:
-                    greet(at(a2=lax.rem(a + da, A), x2=lax.rem(section + dx, X)))
+    def greet(target):
+        pl.semaphore_signal(barrier, inc=1, device_id=target, device_id_type=MESH)
+
+    for da in range(A):
+        for dx in range(X):
+            if da or dx:
+                greet(at(a2=lax.rem(a + da, A), x2=lax.rem(section + dx, X)))
     for dr in range(1, R):
         greet(at(r2=lax.rem(r + dr, R)))
     for dc in range(1, C):
@@ -133,15 +112,21 @@
 
     def first(j, n, a2):
         src = (k_ref, v_ref, q_ref)[n].at[:, cols((a2 * hp + j) * d, d)]
-        remote(src, landing(j, n).at[own_rows(a)], x_send, x_recv.at[j, n, own_half], at(a2=a2)).start()
+        remote(src, landing(j, n).at[own_rows(a)], x_send, x_recv.at[j, H if n == 2 else own_half], at(a2=a2)).start()
 
     def first_own(j, n):
         src = (k_ref, v_ref, q_ref)[n].at[:, cols((a * hp + j) * d, d)]
-        pltpu.make_async_copy(src, landing(j, n).at[own_rows(a)], x_recv.at[j, n, own_half]).start()
+        pltpu.make_async_copy(src, landing(j, n).at[own_rows(a)], x_recv.at[j, H if n == 2 else own_half]).start()
 
     def first_text(a2):
         remote(t_ref.at[:, cols(a2 * width, width)], tb.at[slot, a], t_send, t_recv, at(a2=a2)).start()
 
+    staged = [(tk_hbm, tk_ref), (tv_hbm, tv_ref), (order_hbm, order_ref), (pick_hbm, pick_ref)]
+    staged = [pltpu.make_async_copy(src, dst, early_sem.at[i]) for i, (src, dst) in enumerate(staged)]
+    for copy in staged:
+        copy.start()
+    for copy in staged:
+        copy.wait()
     count = tk_ref.shape[0]
     if 2 * count < wide.shape[0]:
         wide[...] = jnp.zeros_like(wide)
@@ -153,15 +138,7 @@
     for n in range(3):
         first_own(0, n)
 
-    if staged:
-        pl.semaphore_wait(barrier, beside + R - 1 + C - 1)
-    else:
-        pl.semaphore_wait(barrier, A * X - 1 + R - 1 + C - 1)
-    for k in range(1, hops + 1):
-        if staged and k > 1:
-            pl.semaphore_wait(entry.at[k - 2], beside)
-        if staged and k < hops:
-            each(1, lambda a2: greet(at(a2=a2), entry.at[k - 1]))
+    pl.semaphore_wait(barrier, A * X - 1 + R - 1 + C - 1)
 
     def send_all(j, which):
         for n in which:
@@ -181,12 +158,10 @@
             send_all(j + 1, (0, 1))
         send_all(j, (2,))
 
-    pick_copy = pltpu.make_async_copy(pick_hbm, pick_ref, local_sem)
-    pick_copy.start()
     for j in range(hp):
         for b in range(X * A):
             pltpu.make_async_copy(
-                w_hbm.at[pl.ds((b * hp + j) * d, d)], wb.at[j, pl.ds(b * d, d)], w_sem.at[j]
+                w_hbm.at[pl.ds((b * hp + j) * d, d)], wb.at[j, pl.ds(b * d, d)], w_sem
             ).start()
 
     def members():
@@ -219,57 +194,48 @@
                 n = base + (dr - 1) * (C - 1) + dc - 1
                 drain(block(lax.rem(r - dr + R, R) * C + from_core), recv.at[n])
 
-    def kv_block(j, n, h):
-        return lambda s: kv.at[j, n, s, half_rows(h)]
+    def kv_block(j, h):
+        return lambda s: kv.at[j, :, s, half_rows(h)]
 
     def text_block(s):
         return tb.at[s]
 
-    def kv_sems(j, n, h):
-        return kv2_send, kv2_recv.at[j, n, h]
-
     def share_kv(j, h):
-        for n in range(2):
-            drain(kv.at[j, n, slot, half_rows(h)], x_recv.at[j, n, h])
-            share(kv_block(j, n, h), *kv_sems(j, n, h))
+        drain(kv.at[j, :, slot, half_rows(h)], x_recv.at[j, h])
+        share(kv_block(j, h), kv2_send, kv2_recv.at[j, h])
 
     def forward_kv(j, h):
-        for n in range(2):
-            forward(kv_block(j, n, h), *kv_sems(j, n, h))
+        forward(kv_block(j, h), kv2_send, kv2_recv.at[j, h])
 
     def collect_kv(j):
         for h in halves:
-            for n in range(2):
-                collect(kv_block(j, n, h), kv_sems(j, n, h)[1])
+            collect(kv_block(j, h), kv2_recv.at[j, h])
 
     def wait_q(j):
-        for h in halves:
-            drain(qb.at[j, half_rows(h)], x_recv.at[j, 2, h])
-
-    def project(j, parts):
-        for g in parts:
-            drain(att.at[j, :, pl.ds(0, X * group * d)], o_recv.at[j, g])
+        drain(qb.at[j], x_recv.at[j, H])
+
+    def project(j, parts, first_term, last_term):
         columns = o_ref.shape[1]
         step = 768 if columns % 768 == 0 else d
-        if len(parts) == G:
+        if parts is None:
+            drain(att.at[j], o_recv.at[j])
             pieces = [pl.ds(0, X * A * d)]
         else:
-            pieces = [cols((x * A + g * group) * d, group * d) for g in parts for x in range(X)]
-
-        def run(first_term, last_term):
-            @pl.loop(0, columns // step)
-            def _(i):
-                part = pl.ds(pl.multiple_of(i * step, d), step)
-                term = None if first_term else acc[:, part]
-                for piece in pieces:
-                    got = jnp.dot(att[j, :, piece], wb[j, piece, part], preferred_element_type=jnp.float32)
-                    term = got if term is None else term + got
-                if last_term:
-                    o_ref[:, part] = term.astype(o_ref.dtype)
-                else:
-                    acc[:, part] = term
-
-        return run
+            for h in parts:
+                drain(att.at[j, :, pl.ds(0, X * HB * d)], o_recv.at[j + h])
+            pieces = [cols((x * A + h * HB) * d, HB * d) for h in parts for x in range(X)]
+
+        @pl.loop(0, columns // step)
+        def _(i):
+            part = pl.ds(pl.multiple_of(i * step, d), step)
+            term = None if first_term else acc[:, part]
+            for piece in pieces:
+                got = jnp.dot(att[j, :, piece], wb[j, piece, part], preferred_element_type=jnp.float32)
+                term = got if term is None else term + got
+            if last_term:
+                o_ref[:, part] = term.astype(o_ref.dtype)
+            else:
+                acc[:, part] = term
 
     scale = math.log2(math.e) * d ** (-0.5)
     nt = (((1,), (1,)), ((), ()))
@@ -312,7 +278,7 @@
             ob.at[j, own_rows(a2)],
             att.at[j, :, column],
             o_send,
-            o_recv.at[j, own],
+            o_recv.at[j + own_half if j == hp - 1 else j],
             at(a2=a2, x2=lax.rem(section + dx, X)),
         ).start()
 
@@ -328,16 +294,13 @@
 
             @pl.when(a2 == a)
             def _():
-                pltpu.make_async_copy(ob.at[j, own_rows(a2)], att.at[j, :, column], o_recv.at[j, own]).start()
+                pltpu.make_async_copy(ob.at[j, own_rows(a2)], att.at[j, :, column], o_recv.at[j + own_half if j == hp - 1 else j]).start()
 
     def tile_at(k):
         if G & (G - 1):
             return lax.rem(own + 1 + k, G)
         across = jnp.where(own < G // 2, G - 1 - k, k)
         return jnp.where(k < G // 2, across, own ^ (G - 1 - k))
-
-    def part_at(k):
-        return lax.rem(own + k, G) if G & (G - 1) else own ^ k
 
     def attention(j):
         attend(j)
@@ -357,7 +320,6 @@
     for h in halves:
         forward_kv(0, h)
     collect(text_block, t2_recv)
-    pick_copy.wait()
     block = tb[...].reshape(-1, width)
     for n in range(2):
         got = jnp.dot(pick_ref[n], block, preferred_element_type=jnp.float32).astype(jnp.bfloat16)
@@ -373,10 +335,9 @@
         if j + 2 < hp:
             for h in halves:
                 share_kv(j + 2, h)
+    drain(wb, w_sem)
     for j in range(hp - 1):
-        drain(wb.at[j], w_sem.at[j])
-        project(j, list(range(G)))(j == 0, False)
-    drain(wb.at[hp - 1], w_sem.at[hp - 1])
+        project(j, None, j == 0, False)
     others = R * C - 1
     if others:
         drain(kv.at[:, :, pl.ds(0, others)], kv2_send)
@@ -385,11 +346,8 @@
         for n in range(3):
             drain(qb.at[:, pl.ds(0, (A - 1) * rows)], x_send)
         drain(tb.at[slot, pl.ds(0, A - 1)], t_send)
-    if G % 2:
-        project(hp - 1, list(range(G)))(hp == 1, True)
-    else:
-        project(hp - 1, [part_at(k) for k in range(G // 2)])(hp == 1, False)
-        project(hp - 1, [part_at(k) for k in range(G // 2, G)])(False, True)
+    for k, h in enumerate(halves):
+        project(hp - 1, [h], hp == 1 and k == 0, k == H - 1)
     if A * X > 1:
         drain(att.at[:, :, pl.ds(0, (A * X - 1) * d)], o_send)
 
@@ -416,14 +374,14 @@
     pick = jnp.asarray(pick, bf16)
     out_columns = out_weight.shape[1]
     shares = R - 1 + C - 1 + (R - 1) * (C - 1)
-    Y = H = group = 2 if A % 2 == 0 else 1
+    H = group = 2 if A % 2 == 0 else 1
     vmem = pl.BlockSpec(memory_space=pltpu.VMEM)
     hbm = pl.BlockSpec(memory_space=pl.ANY)
     dma = pltpu.SemaphoreType.DMA
     return pl.pallas_call(
-        functools.partial(kernel, (A, R, C, X, hp, Y, H, group)),
+        functools.partial(kernel, (A, R, C, X, hp, H, group)),
         out_shape=pltpu.VMEM((rows, out_columns), bf16),
-        in_specs=[pl.BlockSpec(memory_space=pltpu.SMEM)] + [hbm] * 3 + [vmem] * 3 + [hbm] * 2,
+        in_specs=[pl.BlockSpec(memory_space=pltpu.SMEM)] + [hbm] * 8,
         out_specs=vmem,
         scratch_shapes=[
             pltpu.VMEM((hp, A * rows, HEAD_DIM), bf16),
@@ -436,22 +394,25 @@
             pltpu.VMEM((rows, out_columns), jnp.float32),
             pltpu.VMEM(pick.shape, bf16),
             pltpu.VMEM((A * rows, R * C * A * rows), jnp.float32),
+            pltpu.VMEM(text_keys.shape, bf16),
+            pltpu.VMEM(text_values.shape, bf16),
+            pltpu.VMEM((1, text), jnp.int32),
             pltpu.VMEM((pad, columns), jnp.float32),
             pltpu.VMEM((pad, columns), bf16),
             pltpu.VMEM((pad, columns), bf16),
             dma,
-            dma((hp,)),
-            dma,
-            dma((hp, 3, H)),
-            dma,
-            dma,
-            dma,
-            dma((hp, A // group)),
-            dma,
-            dma((hp, 2, H, shares)),
+            dma((4,)),
+            dma,
+            dma,
+            dma((hp, H + 1)),
+            dma,
+            dma,
+            dma,
+            dma((hp - 1 + H,)),
+            dma,
+            dma((hp, H, shares)),
             dma,
             dma((shares,)),
-            pltpu.SemaphoreType.REGULAR((A,)),
         ],
         compiler_params=pltpu.CompilerParams(
             collective_id=0, has_side_effects=True, vmem_limit_bytes=60 * 1024 * 1024

time: 56.9 us -> 55.9 us (0.982)
  Pallas kernels: 55.3 us -> 54.3 us
    pallas_call x1, Pallas kernels: 55.3 us -> 54.3 us  [shards(): pl.pallas_call(functools.partial(kernel, (A, R, C, X, hp, H, group)), out...]
where the time goes in v2:
time: 55.9 us; the launch traced here: 55.7 us
  Pallas kernels  54.3 us (97%)
  local copies, waits for them, and re-layouts  0.78 us (1%)
  between operations  0.66 us (1%)
    pallas_call x1, Pallas kernels, shards(): pl.pallas_call(functools.partial(kernel, (A, R, C, X, hp, H, group)), out...  54.3 us

profile of v2, /device:TPU:1, one launch (start us, length us, event | category | flops | bytes accessed | tf_op | source)
XLA Modules:
  0.0 55.7 jit_solution(9132150546749811484)
XLA Ops:
  0.7 54.3 %shard_map.91 = bf16[80,3072]{1,0:T(8,128)(2,1)S(1)} custom-call(s32[1]{0:T(128)S(6)} %copy.12.length_ref, bf16[80,3072]{1,0:T(8,128)(2,1)} %q_ref.1, bf16[80,3072]{1,0:T(8,128)(2,1)} %k_ref.1, bf16[80,3072]{1,0:T(8,128)(2,1)} %v_ref.1, bf16[4,3072]{1,0:T(4,128)(2,1)} %tk_hbm.1, bf16[4,3072]{1,0:T(4,128)(2,1)} %tv_hbm.1, s32[1,128]{1,0:T(1,128)} %constant.5.clone.order_hbm, ...), custom_call_target="tpu_custom_call" | custom-call | tf_op jit(solution)/shard_map/pallas_call | solution.py:381
  55.0 0.8 %copy.11 = bf16[80,3072]{1,0:T(8,128)(2,1)} copy(bf16[80,3072]{1,0:T(8,128)(2,1)S(1)} %shard_map.91) | data formatting | bytes 983040
